TPU v7x, 256 devices: a whole 4x4x8 slice. The times are simulated.
256 devices in a mesh: seq: 32 (over x, y, core), tensor: 8 (over z).
Axes of the slice: x: 4, y: 4, z: 8, core: 2. Of those that a mesh axis runs over, the one named last changes fastest.
Arguments:
- tokens: bfloat16 [16384, 4096], P('seq', 'tensor'), may hold values from -6 to 6
- norm_gain: float32 [4096], replicated, may hold values from 0.1 to 1.9
- w_query: bfloat16 [4096, 4096], P('seq', 'tensor'), may hold values from -0.09375 to 0.09375
- w_key: bfloat16 [4096, 4096], P('seq', 'tensor'), may hold values from -0.09375 to 0.09375
- w_value: bfloat16 [4096, 4096], P('seq', 'tensor'), may hold values from -0.09375 to 0.09375
- out_gain: float32 [4096], P('tensor'), may hold values from 0.1 to 1.9
- carried: float32 [32, 128, 128], P('tensor'), may hold values from -384 to 384
Outputs:
- attended: bfloat16 [16384, 4096], P('seq', 'tensor')
- final_state: float32 [32, 128, 128], P('tensor')
All inputs are finite; a program needn't handle non-finite values.
Results may differ from a plain program's by a relative error of at most 0.009.
Values may be sent and summed in bfloat16 or wider, within the bound.
No kernel may reach another device: no remote copies, remote signals or barrier semaphores. Data moves between devices by JAX's collectives and lax.ppermute only.
A program may use at most 64 MiB of HBM per device.

v0:
```python
import jax
import jax.numpy as jnp
from jax import lax
from jax.sharding import PartitionSpec as P

BLOCK = 512


def add_rows(normed, pieces):
    return tuple((jnp.dot(normed, piece, preferred_element_type=jnp.float32) for piece in pieces))


def shards(tokens, norm_gain, w_query, w_key, w_value, out_gain, carried):
    whole = lax.all_gather(tokens, "tensor", axis=1, tiled=True)
    xf = whole.astype(jnp.float32)
    normed = (xf * lax.rsqrt(jnp.mean(xf * xf, axis=1, keepdims=True) + 1e-05) * norm_gain).astype(
        jnp.bfloat16
    )
    rows = normed.shape[0]
    width = w_query.shape[1]
    size = carried.shape[1]
    heads = width // size
    qsum, ksum, vsum = add_rows(
        normed,
        (
            lax.all_gather(w_query, "seq", axis=0, tiled=True),
            lax.all_gather(w_key, "seq", axis=0, tiled=True),
            lax.all_gather(w_value, "seq", axis=0, tiled=True),
        ),
    )
    blocks = rows // BLOCK
    query = qsum.astype(jnp.bfloat16).reshape(blocks, BLOCK, heads, size)
    key = ksum.astype(jnp.bfloat16).reshape(blocks, BLOCK, heads, size)
    value = vsum.astype(jnp.bfloat16).reshape(blocks, BLOCK, heads, size)
    block_state = jnp.einsum("nthd,nthe->nhde", key, value, preferred_element_type=jnp.float32)
    local_total = jnp.sum(block_state, axis=0)
    zero_state = jnp.zeros_like(local_total)
    mine = lax.axis_index("seq")
    piece = lax.all_gather(
        local_total[None].astype(jnp.bfloat16), "seq", axis=0, tiled=True
    ).astype(jnp.float32)
    where = jnp.arange(piece.shape[0], dtype=jnp.int32)
    keep = (where < mine).astype(jnp.float32)
    before = zero_state + jnp.sum(keep[:, None, None, None] * piece, axis=0)
    total = zero_state + jnp.sum(piece, axis=0)
    start_state = carried + before
    running = jnp.cumsum(block_state, axis=0) - block_state
    priors = start_state[None] + running
    inter = jnp.einsum(
        "nthd,nhde->nthe", query.astype(jnp.float32), priors, precision=lax.Precision.HIGHEST
    )
    causal = jnp.tril(jnp.ones((BLOCK, BLOCK), jnp.float32))
    scores = jnp.einsum("nthd,nshd->nhts", query, key, preferred_element_type=jnp.float32)
    weights = (scores * causal).astype(jnp.bfloat16)
    intra = jnp.einsum("nhts,nshe->nthe", weights, value, preferred_element_type=jnp.float32)
    raw = inter + intra
    normal = (
        raw
        * lax.rsqrt(jnp.mean(raw * raw, axis=3, keepdims=True) + 1e-06)
        * out_gain.reshape(heads, size)
    )
    attended = normal.astype(jnp.bfloat16).reshape(rows, width)
    return (attended, carried + total)


def solution(mesh):
    return jax.shard_map(
        shards,
        mesh=mesh,
        in_specs=(
            P("seq", "tensor"),
            P(),
            P("seq", "tensor"),
            P("seq", "tensor"),
            P("seq", "tensor"),
            P("tensor"),
            P("tensor", None, None),
        ),
        out_specs=(P("seq", "tensor"), P("tensor", None, None)),
        check_vma=False,
    )
```

profile of v0, /device:TPU:1, one launch (start us, length us, event | category | flops | bytes accessed | tf_op | source)
XLA Modules:
  0.0 293.1 jit_solution(6839959478735101237)
XLA Ops:
  7.2 0.0 copy-start.4
  7.2 0.0 all-gather.7.cloned.1.call-start
  7.2 0.7 all-gather.7.cloned.1.call-update
  7.9 0.0 all-gather.9.cloned.1.call-start
  8.0 0.7 all-gather.9.cloned.1.call-update
  8.7 0.0 all-gather.11.cloned.1.call-start
  8.7 0.7 all-gather.11.cloned.1.call-update
  9.4 0.0 all-gather.13.cloned.1.call-start
  9.4 0.5 all-gather.13.cloned.1.call-update
  10.0 0.0 all-gather.15.cloned.1.call-start
  10.0 58.4 %all-gather.7.cloned.1.call-done = bf16[512,4096]{1,0:T(8,128)(2,1)} async-done(((bf16[512,512]{1,0:T(8,128)(2,1)}), bf16[512,4096]{1,0:T(8,128)(2,1)}) %all-gather.7.cloned.1.call-update) | async-done | bytes 4194320 | tf_op jit(solution)/shard_map/all_gather | solution.py:14
  68.5 3.1 %fusion = f32[512]{0:T(512)S(1)} fusion(bf16[512,4096]{1,0:T(8,128)(2,1)} %all-gather.7.cloned.1.call-done), kind=kLoop, calls=%fused_computation.4 | loop fusion | flops 6290944 | bytes 4196352 | tf_op jit(solution)/shard_map/reduce_sum | solution.py:16
  71.5 49.6 %all-gather.9.cloned.1.call-done = bf16[4096,512]{1,0:T(8,128)(2,1)} async-done(((bf16[128,512]{1,0:T(8,128)(2,1)}), bf16[4096,512]{1,0:T(8,128)(2,1)}) %all-gather.9.cloned.1.call-update) | async-done | bytes 4194320 | tf_op jit(solution)/shard_map/all_gather | solution.py:27
  121.2 0.0 copy-done.4
  121.2 5.9 %convolution_convert_fusion.2 = bf16[512,512]{0,1:T(8,128)(2,1)S(1)} fusion(bf16[4096,512]{1,0:T(8,128)(2,1)} %all-gather.9.cloned.1.call-done, bf16[512,4096]{1,0:T(8,128)(2,1)} %all-gather.7.cloned.1.call-done, f32[4096]{0:T(1024)S(1)} %copy-done.4, f32[512]{0:T(512)S(1)} %add_rsqrt_fusion.1), kind=kOutput, calls=%fused_computation.14 | convolution fusion | flops 2156134400 | bytes 8931328 | tf_op jit(solution)/shard_map/dot_general | solution.py:10
  127.1 47.2 %all-gather.11.cloned.1.call-done = bf16[4096,512]{1,0:T(8,128)(2,1)} async-done(((bf16[128,512]{1,0:T(8,128)(2,1)}), bf16[4096,512]{1,0:T(8,128)(2,1)}) %all-gather.11.cloned.1.call-update) | async-done | bytes 4194320 | tf_op jit(solution)/shard_map/all_gather | solution.py:28
  174.3 5.9 %convolution_convert_fusion.1 = bf16[512,512]{0,1:T(8,128)(2,1)S(1)} fusion(bf16[4096,512]{1,0:T(8,128)(2,1)} %all-gather.11.cloned.1.call-done, bf16[512,4096]{1,0:T(8,128)(2,1)} %all-gather.7.cloned.1.call-done, f32[4096]{0:T(1024)S(1)} %copy-done.4, f32[512]{0:T(512)S(1)} %add_rsqrt_fusion.1), kind=kOutput, calls=%fused_computation.13 | convolution fusion | flops 2156134400 | bytes 8931328 | tf_op jit(solution)/shard_map/dot_general | solution.py:10
  180.2 1.0 fusion.13
  181.3 0.0 all-gather.15.cloned.1.call-update
  181.3 0.1 fusion.6
  181.4 45.8 %all-gather.13.cloned.1.call-done = bf16[4096,512]{1,0:T(8,128)(2,1)} async-done(((bf16[128,512]{1,0:T(8,128)(2,1)}), bf16[4096,512]{1,0:T(8,128)(2,1)}) %all-gather.13.cloned.1.call-update) | async-done | bytes 4194320 | tf_op jit(solution)/shard_map/all_gather | solution.py:26
  227.2 6.7 %convolution_convert_fusion = bf16[512,512]{0,1:T(8,128)(2,1)} fusion(bf16[4096,512]{1,0:T(8,128)(2,1)} %all-gather.13.cloned.1.call-done, bf16[512,4096]{1,0:T(8,128)(2,1)} %all-gather.7.cloned.1.call-done, f32[4096]{0:T(1024)S(1)} %copy-done.4, f32[512]{0:T(512)S(1)} %add_rsqrt_fusion.1), kind=kOutput, calls=%fused_computation.12 | convolution fusion | flops 2156134400 | bytes 8931328 | tf_op jit(solution)/shard_map/dot_general | solution.py:10
  234.0 0.0 copy-start.1
  234.0 2.5 fusion.4
  236.5 0.0 copy-start
  236.5 0.0 copy-start.2
  236.5 0.0 copy-start.3
  236.5 43.7 %all-gather.15.cloned.1.call-done = bf16[128,128,128]{2,1,0:T(8,128)(2,1)} async-done(((bf16[4,128,128]{2,1,0:T(8,128)(2,1)}), bf16[128,128,128]{2,1,0:T(8,128)(2,1)}) %all-gather.15.cloned.1.call-update) | async-done | bytes 4194320 | tf_op jit(solution)/shard_map/all_gather | solution.py:39
  280.2 3.6 %convert_reduce_fusion = (f32[4,128,128]{2,1,0:T(8,128)S(1)}, f32[4,128,128]{2,1,0:T(8,128)S(1)}) fusion(bf16[32,4,128,128]{3,2,1,0:T(8,128)(2,1)} %bitcast.20, f32[32]{0:T(128)S(1)} %compare_convert_fusion), kind=kLoop, calls=%fused_computation | loop fusion | flops 8257536 | bytes 4718720 | tf_op jit(solution)/shard_map/reduce_sum | solution.py:45
  283.8 0.0 copy-done.1
  283.8 0.0 copy-done
  283.9 0.0 copy-done.2
  283.9 0.7 multiply_reduce_fusion
  284.6 0.0 copy-done.3
  284.6 0.2 multiply_convert_fusion.1
  284.8 1.0 copy.16
  285.8 0.7 add.52
  (3 shorter events, 0.0 us)
Async XLA Ops:
  7.2 114.0 %copy-start.4 = (f32[4096]{0:T(1024)S(1)}, f32[4096]{0:T(1024)}, u32[]{:S(2)}) copy-start(f32[4096]{0:T(1024)} %param.8) | copy-start | bytes 49156
  7.2 61.3 %all-gather.7.cloned.1.call-start = ((), (), s32[]{:S(2)}) async-start(), calls=%async_computation | async-start | bytes 4718592 | tf_op jit(solution)/shard_map/all_gather | solution.py:14
  7.9 113.2 %all-gather.9.cloned.1.call-start = ((), (), s32[]{:S(2)}) async-start(), calls=%async_computation.1 | async-start | bytes 4325376 | tf_op jit(solution)/shard_map/all_gather | solution.py:27
  8.7 165.6 %all-gather.11.cloned.1.call-start = ((), (), s32[]{:S(2)}) async-start(), calls=%async_computation.2 | async-start | bytes 4325376 | tf_op jit(solution)/shard_map/all_gather | solution.py:28
  9.4 217.8 %all-gather.13.cloned.1.call-start = ((), (), s32[]{:S(2)}) async-start(), calls=%async_computation.3 | async-start | bytes 4325376 | tf_op jit(solution)/shard_map/all_gather | solution.py:26
  10.0 270.2 %all-gather.15.cloned.1.call-start = ((), (), s32[]{:S(2)}) async-start(), calls=%async_computation.4 | async-start | bytes 4325376 | tf_op jit(solution)/shard_map/all_gather | solution.py:39
  234.0 49.9 %copy-start.1 = (f32[4,128,128]{2,1,0:T(8,128)S(1)}, f32[4,128,128]{2,1,0:T(8,128)}, u32[]{:S(2)}) copy-start(f32[4,128,128]{2,1,0:T(8,128)} %param.13) | copy-start | bytes 786436
  236.5 47.4 %copy-start = (bf16[512,512]{0,1:T(8,128)(2,1)S(1)}, bf16[512,512]{0,1:T(8,128)(2,1)}, u32[]{:S(2)}) copy-start(bf16[512,512]{0,1:T(8,128)(2,1)} %convolution_convert_fusion) | copy-start | bytes 1572868
  236.5 47.4 %copy-start.2 = (f32[4,128,128]{2,1,0:T(8,128)S(1)}, f32[4,128,128]{2,1,0:T(8,128)}, u32[]{:S(2)}) copy-start(f32[4,128,128]{2,1,0:T(8,128)} %get-tuple-element.9) | copy-start | bytes 786436
  236.5 48.1 %copy-start.3 = (f32[512]{0:T(512)S(1)}, f32[512]{0:T(512)}, u32[]{:S(2)}) copy-start(f32[512]{0:T(512)} %param.12) | copy-start | bytes 6148
Sparse Core Ops, SparseCore 0:
  9.8 58.6 all-gather.6
  71.0 50.0 all-gather.8
  123.7 50.5 all-gather.10
  176.7 50.5 all-gather.12
  229.6 50.5 all-gather.14
where the time goes:
time: 293 us
  waiting for transfers between devices  247 us (84%)
  matrix products  22.9 us (8%)
  between operations  13.9 us (5%)
  other arithmetic  7.74 us (3%)
    all_gather x1, waiting for transfers between devices, shards(): whole = lax.all_gather(tokens, 'tensor', axis=1, tiled=True)  58.4 us
    all_gather x1, waiting for transfers between devices, shards(): lax.all_gather(w_key, 'seq', axis=0, tiled=True)  49.6 us
    all_gather x1, waiting for transfers between devices, shards(): lax.all_gather(w_value, 'seq', axis=0, tiled=True)  47.2 us
    all_gather x1, waiting for transfers between devices, shards(): lax.all_gather(w_query, 'seq', axis=0, tiled=True)  45.8 us
    all_gather x1, waiting for transfers between devices, shards(): lax.all_gather(local_total[None].astype(jnp.bfloat16), 'seq', axis=0, til...  43.7 us
    dot_general x3, matrix products, add_rows(): jnp.dot(normed, piece, preferred_element_type=jnp.float32)  18.6 us
  transfers between devices with their start and end apart: 5, of which 5 were waited for; matrix products, arithmetic and copies ran while one was open for 9% of the time, Pallas kernels for 0%

commit v1 on v0

--- a/solution.py
+++ b/solution.py
@@ -11,7 +11,14 @@
 
 
 def shards(tokens, norm_gain, w_query, w_key, w_value, out_gain, carried):
-    whole = lax.all_gather(tokens, "tensor", axis=1, tiled=True)
+    count = lax.axis_size("tensor")
+    right = [(i, (i + 1) % count) for i in range(count)]
+    shards_2 = [tokens]
+    for hop in range(1, count):
+        shards_2 = [lax.ppermute(shards_2[0], "tensor", right), *shards_2]
+    out = jnp.concatenate(shards_2, axis=1)
+    shift = (lax.axis_index("tensor") + 1) * shards_2[-1].shape[1]
+    whole = jnp.roll(out, shift, axis=1)
     xf = whole.astype(jnp.float32)
     normed = (xf * lax.rsqrt(jnp.mean(xf * xf, axis=1, keepdims=True) + 1e-05) * norm_gain).astype(
         jnp.bfloat16

time: 293 us -> 239 us (0.82)
  waiting for transfers between devices: 247 us -> 182 us
  local copies, waits for them, and re-layouts: 1.03 us -> 10.7 us
    ppermute x0 -> x7, waiting for transfers between devices: none -> 85.2 us  [shards(): shards_2 = [lax.ppermute(shards_2[0], 'tensor', right), *shards_2]]
    all_gather x1 -> x0, waiting for transfers between devices: 58.4 us -> none  [shards(): whole = lax.all_gather(tokens, 'tensor', axis=1, tiled=True)]
    all_gather x1, waiting for transfers between devices: 49.6 us -> 0.02 us  [shards(): lax.all_gather(w_key, 'seq', axis=0, tiled=True)]
    all_gather x1, waiting for transfers between devices: 47.2 us -> 4.86 us  [shards(): lax.all_gather(w_value, 'seq', axis=0, tiled=True)]
    unnamed x11 -> x26, local copies, waits for them, and re-layouts: 1.03 us -> 10.6 us
  transfers between devices with their start and end apart: 5 -> 11, of which waited for: 5 -> 10; matrix products, arithmetic and copies ran while one was open for 9% -> 12% of each run, Pallas kernels for 0% -> 0%
where the time goes in v1:
time: 239 us
  waiting for transfers between devices  182 us (76%)
  matrix products  24.1 us (10%)
  between operations  14 us (6%)
  local copies, waits for them, and re-layouts  10.7 us (4%)
  other arithmetic  5.54 us (2%)
  starting transfers between devices  2.71 us (1%)
    ppermute x7, waiting for transfers between devices, shards(): shards_2 = [lax.ppermute(shards_2[0], 'tensor', right), *shards_2]  85.2 us
    all_gather x1, waiting for transfers between devices, shards(): lax.all_gather(w_query, 'seq', axis=0, tiled=True)  46 us
    all_gather x1, waiting for transfers between devices, shards(): lax.all_gather(local_total[None].astype(jnp.bfloat16), 'seq', axis=0, til...  43.8 us
    dot_general x3, matrix products, add_rows(): jnp.dot(normed, piece, preferred_element_type=jnp.float32)  18.8 us
    unnamed x26, local copies, waits for them, and re-layouts  10.6 us
    all_gather x1, waiting for transfers between devices, shards(): lax.all_gather(w_value, 'seq', axis=0, tiled=True)  4.86 us
  transfers between devices with their start and end apart: 11, of which 10 were waited for; matrix products, arithmetic and copies ran while one was open for 12% of the time, Pallas kernels for 0%

profile of v1, /device:TPU:1, one launch (start us, length us, event | category | flops | bytes accessed | tf_op | source)
XLA Modules:
  0.0 239.0 jit_solution(12148023381970950608)
XLA Ops:
  7.2 0.0 all-gather.6.cloned.1.call-start
  7.2 0.7 all-gather.6.cloned.1.call-update
  7.9 0.0 all-gather.8.cloned.1.call-start
  8.0 0.7 all-gather.8.cloned.1.call-update
  8.7 0.0 all-gather.10.cloned.1.call-start
  8.7 0.7 all-gather.10.cloned.1.call-update
  9.4 0.0 all-gather.12.cloned.1.call-start
  9.4 2.5 %collective-permute-start = (bf16[512,512]{1,0:T(8,128)(2,1)}, bf16[512,512]{1,0:T(8,128)(2,1)S(1)}, u32[]{:S(2)}, u32[]{:S(2)}) collective-permute-start(bf16[512,512]{1,0:T(8,128)(2,1)} %param.7), channel_id=1, source_target_pairs={{0,1},{1,2},{2,3},{3,4},{4,5},{5,6},{6,7},{7,0},{8,9},{9,10},{10,1... | collective-permute-start | bytes 1572872 | tf_op jit(solution)/shard_map/ppermute | solution.py:18
  12.0 15.8 %collective-permute-done = bf16[512,512]{1,0:T(8,128)(2,1)S(1)} collective-permute-done((bf16[512,512]{1,0:T(8,128)(2,1)}, bf16[512,512]{1,0:T(8,128)(2,1)S(1)}, u32[]{:S(2)}, u32[]{:S(2)}) %collective-permute-start) | collective-permute-done | bytes 524320 | tf_op jit(solution)/shard_map/ppermute | solution.py:18
  27.8 13.4 %collective-permute-done.1 = bf16[512,512]{1,0:T(8,128)(2,1)S(1)} collective-permute-done((bf16[512,512]{1,0:T(8,128)(2,1)S(1)}, bf16[512,512]{1,0:T(8,128)(2,1)S(1)}, u32[]{:S(2)}, u32[]{:S(2)}) %collective-permute-start.1) | collective-permute-done | bytes 524320 | tf_op jit(solution)/shard_map/ppermute | solution.py:18
  41.2 12.6 %collective-permute-done.2 = bf16[512,512]{1,0:T(8,128)(2,1)S(1)} collective-permute-done((bf16[512,512]{1,0:T(8,128)(2,1)S(1)}, bf16[512,512]{1,0:T(8,128)(2,1)S(1)}, u32[]{:S(2)}, u32[]{:S(2)}) %collective-permute-start.2) | collective-permute-done | bytes 524320 | tf_op jit(solution)/shard_map/ppermute | solution.py:18
  53.8 11.7 %collective-permute-done.3 = bf16[512,512]{1,0:T(8,128)(2,1)S(1)} collective-permute-done((bf16[512,512]{1,0:T(8,128)(2,1)S(1)}, bf16[512,512]{1,0:T(8,128)(2,1)S(1)}, u32[]{:S(2)}, u32[]{:S(2)}) %collective-permute-start.3) | collective-permute-done | bytes 524320 | tf_op jit(solution)/shard_map/ppermute | solution.py:18
  65.4 10.7 %collective-permute-done.4 = bf16[512,512]{1,0:T(8,128)(2,1)S(1)} collective-permute-done((bf16[512,512]{1,0:T(8,128)(2,1)S(1)}, bf16[512,512]{1,0:T(8,128)(2,1)S(1)}, u32[]{:S(2)}, u32[]{:S(2)}) %collective-permute-start.4) | collective-permute-done | bytes 524320 | tf_op jit(solution)/shard_map/ppermute | solution.py:18
  76.2 10.5 %collective-permute-done.5 = bf16[512,512]{1,0:T(8,128)(2,1)} collective-permute-done((bf16[512,512]{1,0:T(8,128)(2,1)S(1)}, bf16[512,512]{1,0:T(8,128)(2,1)}, u32[]{:S(2)}, u32[]{:S(2)}) %collective-permute-start.5) | collective-permute-done | bytes 524320 | tf_op jit(solution)/shard_map/ppermute | solution.py:18
  86.7 10.6 %collective-permute-done.6 = bf16[512,512]{1,0:T(8,128)(2,1)} collective-permute-done((bf16[512,512]{1,0:T(8,128)(2,1)}, bf16[512,512]{1,0:T(8,128)(2,1)}, u32[]{:S(2)}, u32[]{:S(2)}) %collective-permute-start.6) | collective-permute-done | bytes 524320 | tf_op jit(solution)/shard_map/ppermute | solution.py:18
  97.2 1.1 constant_dynamic-update-slice_fusion.15
  98.4 1.1 constant_dynamic-update-slice_fusion.14
  99.5 0.1 constant_dynamic-update-slice_fusion.13
  99.6 0.1 constant_dynamic-update-slice_fusion.12
  99.6 0.1 constant_dynamic-update-slice_fusion.11
  99.7 0.1 constant_dynamic-update-slice_fusion.10
  99.8 0.1 constant_dynamic-update-slice_fusion.9
  99.9 1.1 constant_dynamic-update-slice_fusion.8
  101.0 1.1 constant_dynamic-update-slice_fusion.7
  102.1 1.2 constant_dynamic-update-slice_fusion.6
  103.3 0.1 constant_dynamic-update-slice_fusion.5
  103.4 0.1 constant_dynamic-update-slice_fusion.4
  103.5 0.1 constant_dynamic-update-slice_fusion.3
  103.6 0.1 constant_dynamic-update-slice_fusion.2
  103.6 0.1 constant_dynamic-update-slice_fusion.1
  103.7 0.1 constant_dynamic-update-slice_fusion
  103.8 3.2 %copy-done = bf16[512,8192]{1,0:T(8,128)(2,1)} copy-done((bf16[512,8192]{1,0:T(8,128)(2,1)}, bf16[512,8192]{1,0:T(8,128)(2,1)S(1)}, u32[]{:S(2)}) %copy-start) | copy-done | bytes 8388632
  107.0 0.9 fusion
  107.9 0.0 all-gather.6.cloned.1.call-done
  108.0 6.2 %convolution_convert_fusion.2 = bf16[512,512]{0,1:T(8,128)(2,1)S(1)} fusion(bf16[4096,512]{1,0:T(8,128)(2,1)} %all-gather.6.cloned.1.call-done, f32[4096]{0:T(1024)S(1)} %copy-done.4, f32[512]{0:T(512)S(1)} %add_rsqrt_fusion.1, bf16[512,8192]{1,0:T(8,128)(2,1)} %copy-done, s32[]{:T(128)S(6)} %select_n.22), kind=kOutput, calls=%fused_computation.14 | convolution fusion | flops 2156134400 | bytes 8931332 | tf_op jit(solution)/shard_map/dot_general | solution.py:10
  114.1 4.9 %all-gather.8.cloned.1.call-done = bf16[4096,512]{1,0:T(8,128)(2,1)} async-done(((bf16[128,512]{1,0:T(8,128)(2,1)}), bf16[4096,512]{1,0:T(8,128)(2,1)}) %all-gather.8.cloned.1.call-update) | async-done | bytes 4194320 | tf_op jit(solution)/shard_map/all_gather | solution.py:35
  119.0 5.9 %convolution_convert_fusion.1 = bf16[512,512]{0,1:T(8,128)(2,1)S(1)} fusion(bf16[4096,512]{1,0:T(8,128)(2,1)} %all-gather.8.cloned.1.call-done, f32[4096]{0:T(1024)S(1)} %copy-done.4, f32[512]{0:T(512)S(1)} %add_rsqrt_fusion.1, bf16[512,8192]{1,0:T(8,128)(2,1)} %copy-done, s32[]{:T(128)S(6)} %select_n.22), kind=kOutput, calls=%fused_computation.13 | convolution fusion | flops 2156134400 | bytes 8931332 | tf_op jit(solution)/shard_map/dot_general | solution.py:10
  124.9 1.0 fusion.13
  126.0 0.1 fusion.6
  126.2 46.0 %all-gather.10.cloned.1.call-done = bf16[4096,512]{1,0:T(8,128)(2,1)} async-done(((bf16[128,512]{1,0:T(8,128)(2,1)}), bf16[4096,512]{1,0:T(8,128)(2,1)}) %all-gather.10.cloned.1.call-update) | async-done | bytes 4194320 | tf_op jit(solution)/shard_map/all_gather | solution.py:33
  172.1 6.7 %convolution_convert_fusion = bf16[512,512]{0,1:T(8,128)(2,1)} fusion(bf16[4096,512]{1,0:T(8,128)(2,1)} %all-gather.10.cloned.1.call-done, f32[4096]{0:T(1024)S(1)} %copy-done.4, f32[512]{0:T(512)S(1)} %add_rsqrt_fusion.1, bf16[512,8192]{1,0:T(8,128)(2,1)} %copy-done, s32[]{:T(128)S(6)} %select_n.22), kind=kOutput, calls=%fused_computation.12 | convolution fusion | flops 2156134400 | bytes 8931332 | tf_op jit(solution)/shard_map/dot_general | solution.py:10
  178.9 2.4 %fusion.4 = f32[4,128,512]{2,1,0:T(8,128)S(1)} fusion(bf16[512,4,128]{0,2,1:T(8,128)(2,1)S(1)} %bitcast.24, bf16[512,4,128]{0,2,1:T(8,128)(2,1)} %bitcast.25, bf16[512,4,128]{0,2,1:T(8,128)(2,1)S(1)} %bitcast.22, f32[512,512]{1,0:T(8,128)S(1)} %fusion.6), kind=kOutput, calls=%fused_computation.9 | convolution fusion | flops 538968064 | bytes 3670016 | tf_op jit(solution)/shard_map/nhts,nshe->nthe/dot_general | solution.py:62
  181.3 43.8 %all-gather.12.cloned.1.call-done = bf16[128,128,128]{2,1,0:T(8,128)(2,1)} async-done(((bf16[4,128,128]{2,1,0:T(8,128)(2,1)}), bf16[128,128,128]{2,1,0:T(8,128)(2,1)}) %all-gather.12.cloned.1.call-update) | async-done | bytes 4194320 | tf_op jit(solution)/shard_map/all_gather | solution.py:46
  225.1 3.6 %convert_reduce_fusion = (f32[4,128,128]{2,1,0:T(8,128)S(1)}, f32[4,128,128]{2,1,0:T(8,128)S(1)}) fusion(bf16[32,4,128,128]{3,2,1,0:T(8,128)(2,1)} %bitcast.20, f32[32]{0:T(128)S(1)} %compare_convert_fusion), kind=kLoop, calls=%fused_computation | loop fusion | flops 8257536 | bytes 4718720 | tf_op jit(solution)/shard_map/reduce_sum | solution.py:52
  228.8 1.8 multiply_reduce_fusion
  230.6 0.2 multiply_convert_fusion.1
  230.8 1.0 copy.16
  231.8 0.7 add.68
  (19 shorter events, 0.1 us)
Async XLA Ops:
  7.2 96.6 %copy-start.1 = (bf16[512,512]{1,0:T(8,128)(2,1)S(1)}, bf16[512,512]{1,0:T(8,128)(2,1)}, u32[]{:S(2)}) copy-start(bf16[512,512]{1,0:T(8,128)(2,1)} %param.7) | copy-start | bytes 1572868
  7.2 100.8 %all-gather.6.cloned.1.call-start = ((), (), s32[]{:S(2)}) async-start(), calls=%async_computation | async-start | bytes 4325376 | tf_op jit(solution)/shard_map/all_gather | solution.py:34
  7.9 111.1 %all-gather.8.cloned.1.call-start = ((), (), s32[]{:S(2)}) async-start(), calls=%async_computation.1 | async-start | bytes 4325376 | tf_op jit(solution)/shard_map/all_gather | solution.py:35
  8.7 163.5 %all-gather.10.cloned.1.call-start = ((), (), s32[]{:S(2)}) async-start(), calls=%async_computation.2 | async-start | bytes 4325376 | tf_op jit(solution)/shard_map/all_gather | solution.py:33
  9.4 215.7 %all-gather.12.cloned.1.call-start = ((), (), s32[]{:S(2)}) async-start(), calls=%async_computation.3 | async-start | bytes 4325376 | tf_op jit(solution)/shard_map/all_gather | solution.py:46
  9.4 18.3 %collective-permute-start = (bf16[512,512]{1,0:T(8,128)(2,1)}, bf16[512,512]{1,0:T(8,128)(2,1)S(1)}, u32[]{:S(2)}, u32[]{:S(2)}) collective-permute-start(bf16[512,512]{1,0:T(8,128)(2,1)} %param.7), channel_id=1, source_target_pairs={{0,1},{1,2},{2,3},{3,4},{4,5},{5,6},{6,7},{7,0},{8,9},{9,10},{10,1... | collective-permute-start | bytes 1572872 | tf_op jit(solution)/shard_map/ppermute | solution.py:18
  27.8 13.4 %collective-permute-start.1 = (bf16[512,512]{1,0:T(8,128)(2,1)S(1)}, bf16[512,512]{1,0:T(8,128)(2,1)S(1)}, u32[]{:S(2)}, u32[]{:S(2)}) collective-permute-start(bf16[512,512]{1,0:T(8,128)(2,1)S(1)} %collective-permute-done), channel_id=1, source_target_pairs={{0,1},{1,2},{2,3},{3,4},{4,5},{5,6},{6,7},{7,0},{8,9},{9,10},{10,1... | collective-permute-start | bytes 1572872 | tf_op jit(solution)/shard_map/ppermute | solution.py:18
  41.2 12.6 %collective-permute-start.2 = (bf16[512,512]{1,0:T(8,128)(2,1)S(1)}, bf16[512,512]{1,0:T(8,128)(2,1)S(1)}, u32[]{:S(2)}, u32[]{:S(2)}) collective-permute-start(bf16[512,512]{1,0:T(8,128)(2,1)S(1)} %collective-permute-done.1), channel_id=1, source_target_pairs={{0,1},{1,2},{2,3},{3,4},{4,5},{5,6},{6,7},{7,0},{8,9},{9,10},{10,1... | collective-permute-start | bytes 1572872 | tf_op jit(solution)/shard_map/ppermute | solution.py:18
  53.8 11.7 %collective-permute-start.3 = (bf16[512,512]{1,0:T(8,128)(2,1)S(1)}, bf16[512,512]{1,0:T(8,128)(2,1)S(1)}, u32[]{:S(2)}, u32[]{:S(2)}) collective-permute-start(bf16[512,512]{1,0:T(8,128)(2,1)S(1)} %collective-permute-done.2), channel_id=1, source_target_pairs={{0,1},{1,2},{2,3},{3,4},{4,5},{5,6},{6,7},{7,0},{8,9},{9,10},{10,1... | collective-permute-start | bytes 1572872 | tf_op jit(solution)/shard_map/ppermute | solution.py:18
  65.4 10.7 %collective-permute-start.4 = (bf16[512,512]{1,0:T(8,128)(2,1)S(1)}, bf16[512,512]{1,0:T(8,128)(2,1)S(1)}, u32[]{:S(2)}, u32[]{:S(2)}) collective-permute-start(bf16[512,512]{1,0:T(8,128)(2,1)S(1)} %collective-permute-done.3), channel_id=1, source_target_pairs={{0,1},{1,2},{2,3},{3,4},{4,5},{5,6},{6,7},{7,0},{8,9},{9,10},{10,1... | collective-permute-start | bytes 1572872 | tf_op jit(solution)/shard_map/ppermute | solution.py:18
  76.2 10.5 %collective-permute-start.5 = (bf16[512,512]{1,0:T(8,128)(2,1)S(1)}, bf16[512,512]{1,0:T(8,128)(2,1)}, u32[]{:S(2)}, u32[]{:S(2)}) collective-permute-start(bf16[512,512]{1,0:T(8,128)(2,1)S(1)} %collective-permute-done.4), channel_id=1, source_target_pairs={{0,1},{1,2},{2,3},{3,4},{4,5},{5,6},{6,7},{7,0},{8,9},{9,10},{10,1... | collective-permute-start | bytes 1572872 | tf_op jit(solution)/shard_map/ppermute | solution.py:18
  86.7 10.6 %collective-permute-start.6 = (bf16[512,512]{1,0:T(8,128)(2,1)}, bf16[512,512]{1,0:T(8,128)(2,1)}, u32[]{:S(2)}, u32[]{:S(2)}) collective-permute-start(bf16[512,512]{1,0:T(8,128)(2,1)} %collective-permute-done.5), channel_id=1, source_target_pairs={{0,1},{1,2},{2,3},{3,4},{4,5},{5,6},{6,7},{7,0},{8,9},{9,10},{10,1... | collective-permute-start | bytes 1572872 | tf_op jit(solution)/shard_map/ppermute | solution.py:18
  99.6 8.3 %copy-start.4 = (f32[4096]{0:T(1024)S(1)}, f32[4096]{0:T(1024)}, u32[]{:S(2)}) copy-start(f32[4096]{0:T(1024)} %param.8) | copy-start | bytes 49156
  103.8 3.2 %copy-start = (bf16[512,8192]{1,0:T(8,128)(2,1)}, bf16[512,8192]{1,0:T(8,128)(2,1)S(1)}, u32[]{:S(2)}) copy-start(bf16[512,8192]{1,0:T(8,128)(2,1)S(1)} %constant_dynamic-update-slice_fusion) | copy-start | bytes 25165828
  126.2 102.6 %copy-start.2 = (f32[4,128,128]{2,1,0:T(8,128)S(1)}, f32[4,128,128]{2,1,0:T(8,128)}, u32[]{:S(2)}) copy-start(f32[4,128,128]{2,1,0:T(8,128)} %param.13) | copy-start | bytes 786436
  178.9 51.7 %copy-start.3 = (f32[512]{0:T(512)S(1)}, f32[512]{0:T(512)}, u32[]{:S(2)}) copy-start(f32[512]{0:T(512)} %param.12) | copy-start | bytes 6148
Sparse Core Ops, SparseCore 0:
  10.6 55.2 all-gather.5
  68.5 50.5 all-gather.7
  121.6 50.5 all-gather.9
  174.5 50.5 all-gather.11
